TPU v7x, 256 devices: a whole 4x4x8 slice. The times are simulated.
256 devices in a mesh: dp: 8 (over z), seq: 32 (over x, y, core).
Axes of the slice: x: 4, y: 4, z: 8, core: 2. Of those that a mesh axis runs over, the one named last changes fastest.
Arguments:
- tokens: bfloat16 [8, 4096, 1024], P('dp', 'seq'), may hold values from -6 to 6
- weights: bfloat16 [1024, 3072], replicated, may hold values from -0.1875 to 0.1875
- dout: bfloat16 [8, 4096, 1024], P('dp', 'seq'), may hold values from -6 to 6
Outputs:
- token_grad: bfloat16 [8, 4096, 1024], P('dp', 'seq')
- proj_grad: float32 [1024, 3072], P(('dp', 'seq'))
All inputs are finite; a program needn't handle non-finite values.
Results may differ from a plain program's by a relative error of at most 0.007.
Values sent between devices are 32-bit elements; how exact they have to be, the bound alone decides.
A program may use at most 128 MiB of HBM per device.

v0:
```python
import math

import jax
import jax.numpy as jnp
from jax import lax
from jax.sharding import PartitionSpec as P

HEADS = 8
HD = 128


def entering(part, axis, combine, identity, reverse):
    count = lax.axis_size(axis)
    place = lax.axis_index(axis)
    ahead = count - 1 - place if reverse else place
    gathered = lax.all_gather(part, axis)
    state = jnp.zeros_like(part) + jnp.asarray(identity, part.dtype)

    def one(hop, state):
        source = count - 1 - hop if reverse else hop
        return combine(state, lax.dynamic_index_in_dim(gathered, source, 0, False))

    return lax.fori_loop(0, ahead, one, state)


def add_states(earlier, later):
    return earlier + later


def shards(tokens, weights, dout):
    rows = tokens.shape[1]
    width = tokens.shape[2]
    inner = HEADS * HD
    seq_count = lax.axis_size("seq")
    data_count = lax.axis_size("dp")
    scale = 1.0 / math.sqrt(HD * rows * seq_count)
    factor = 1.0 / math.sqrt(data_count * rows * seq_count)
    flat = tokens.reshape(rows, width)
    proj = jnp.dot(flat, weights, preferred_element_type=jnp.float32).astype(jnp.bfloat16)
    queries = proj[:, :inner].reshape(rows, HEADS, HD)
    keys = proj[:, inner : 2 * inner].reshape(rows, HEADS, HD)
    values = proj[:, 2 * inner :].reshape(rows, HEADS, HD)
    grads_out = dout.reshape(rows, HEADS, HD)
    kv_local = jnp.einsum("thi,thj->hij", keys, values, preferred_element_type=jnp.float32)
    qg_local = scale * jnp.einsum(
        "thi,thj->hij", queries, grads_out, preferred_element_type=jnp.float32
    )
    zeros_state = jnp.zeros_like(kv_local)
    prefix = entering(kv_local, "seq", add_states, zeros_state, False)
    suffix = entering(qg_local, "seq", add_states, zeros_state, True)
    prefix_low = prefix.astype(jnp.bfloat16)
    suffix_low = suffix.astype(jnp.bfloat16)
    position = jnp.arange(rows)
    causal = (position[:, None] >= position[None, :])[None]
    score_a = jnp.where(
        causal,
        jnp.einsum("thj,shj->hts", grads_out, values, preferred_element_type=jnp.float32),
        0.0,
    ).astype(jnp.bfloat16)
    score_b = jnp.where(
        causal, jnp.einsum("thi,shi->hts", queries, keys, preferred_element_type=jnp.float32), 0.0
    ).astype(jnp.bfloat16)
    grad_q = scale * (
        jnp.einsum("hts,shi->thi", score_a, keys, preferred_element_type=jnp.float32)
        + jnp.einsum("thj,hij->thi", grads_out, prefix_low, preferred_element_type=jnp.float32)
    )
    grad_k = scale * jnp.einsum(
        "hts,thi->shi", score_a, queries, preferred_element_type=jnp.float32
    ) + jnp.einsum("shj,hij->shi", values, suffix_low, preferred_element_type=jnp.float32)
    grad_v = scale * jnp.einsum(
        "hts,thj->shj", score_b, grads_out, preferred_element_type=jnp.float32
    ) + jnp.einsum("shi,hij->shj", keys, suffix_low, preferred_element_type=jnp.float32)
    qkv_grad = jnp.concatenate(
        [grad_q.reshape(rows, inner), grad_k.reshape(rows, inner), grad_v.reshape(rows, inner)],
        axis=1,
    ).astype(jnp.bfloat16)
    token_grad = lax.dot_general(
        qkv_grad, weights, (((1,), (1,)), ((), ())), preferred_element_type=jnp.float32
    )
    token_grad = token_grad.astype(jnp.bfloat16).reshape(1, rows, width)
    proj_grad = lax.psum_scatter(
        lax.dot_general(
            flat, qkv_grad, (((0,), (0,)), ((), ())), preferred_element_type=jnp.float32
        )
        * factor,
        ("dp", "seq"),
        scatter_dimension=0,
        tiled=True,
    )
    return (token_grad, proj_grad)


def solution(mesh):
    in_specs = (P("dp", "seq", None), P(), P("dp", "seq", None))
    out_specs = (P("dp", "seq", None), P(("dp", "seq"), None))
    return jax.shard_map(shards, mesh=mesh, in_specs=in_specs, out_specs=out_specs, check_vma=False)
```

profile of v0, /device:TPU:1, one launch (start us, length us, event | category | flops | bytes accessed | tf_op | source)
XLA Modules:
  0.0 512.3 jit_solution(17477586255066074529)
XLA Ops:
  8.4 3.8 convolution_convert_fusion
  16.0 79.3 %all-gather.7.cloned.1.call-done = f32[256,128,128]{2,1,0:T(8,128)} async-done(((f32[8,128,128]{2,1,0:T(8,128)}), f32[256,128,128]{2,1,0:T(8,128)}) %all-gather.7.cloned.1.call-update) | async-done | bytes 16777232 | tf_op jit(solution)/shard_map/all_gather | solution.py:16
  95.3 35.8 %while.23 = (s32[]{:T(128)}, f32[8,128,128]{2,1,0:T(8,128)S(1)}, s32[]{:T(128)}, f32[32,8,128,128]{3,2,1,0:T(8,128)}, s32[]{:T(128)}, /*index=5*/s32[]{:T(128)}, s32[]{:T(128)}, s32[]{:T(128)}) while((s32[]{:T(128)}, f32[8,128,128]{2,1,0:T(8,128)S(1)}, s32[]{:T(128)}, f32[32,8,128,128]{3,2,1,0:T(8,128)}, s32[]{:T(128)}, /*index=5*/s32[]{:T(128)}, ...), condition=%wide.region_3.4_spmd, body=%wide.region_2.3_spmd.sunk | while | flops 131078 | bytes 1573007 | solution.py:23
  95.4 1.2 bitcast_add_fusion.5
  96.6 1.2 bitcast_add_fusion.5
  97.7 1.2 bitcast_add_fusion.5
  98.9 1.2 bitcast_add_fusion.5
  100.1 1.2 bitcast_add_fusion.5
  101.3 1.2 bitcast_add_fusion.5
  102.5 1.2 bitcast_add_fusion.5
  108.5 1.2 bitcast_add_fusion.5
  109.7 1.2 bitcast_add_fusion.5
  114.5 1.2 bitcast_add_fusion.5
  115.7 1.2 bitcast_add_fusion.5
  116.9 1.2 bitcast_add_fusion.5
  118.1 1.2 bitcast_add_fusion.5
  119.3 1.2 bitcast_add_fusion.5
  120.5 1.2 bitcast_add_fusion.5
  121.7 1.2 bitcast_add_fusion.5
  122.9 1.2 bitcast_add_fusion.5
  124.1 1.2 bitcast_add_fusion.5
  125.2 1.2 bitcast_add_fusion.5
  126.4 1.2 bitcast_add_fusion.5
  127.6 1.2 bitcast_add_fusion.5
  128.8 1.2 bitcast_add_fusion.5
  131.9 43.0 %all-gather.5.cloned.1.call-done = f32[256,128,128]{2,1,0:T(8,128)} async-done(((f32[8,128,128]{2,1,0:T(8,128)}), f32[256,128,128]{2,1,0:T(8,128)}) %all-gather.5.cloned.1.call-update) | async-done | bytes 16777232 | tf_op jit(solution)/shard_map/all_gather | solution.py:16
  175.0 1.2 while.22
  175.0 1.2 bitcast_add_fusion.4
  176.4 6.3 %multiply_bitcast_fusion = f32[1024,3072]{0,1:T(8,128)} fusion(bf16[128,1024]{0,1:T(8,128)(2,1)S(1)} %bitcast.86, bf16[128,1024]{0,1:T(8,128)(2,1)S(1)} %bitcast.88, bf16[128,1024]{0,1:T(8,128)(2,1)S(1)} %bitcast.90, bf16[1,128,1024]{2,1,0:T(8,128)(2,1)S(1)} %copy-done), kind=kOutput, calls=%fused_computation.2 | convolution fusion | flops 810811392 | bytes 13631488 | tf_op jit(solution)/shard_map/dot_general | solution.py:82
  182.7 5.7 %fusion.9 = bf16[1,128,1024]{2,1,0:T(8,128)(2,1)} fusion(bf16[1024,3072]{1,0:T(8,128)(2,1)} %param.8, bf16[128,1024]{0,1:T(8,128)(2,1)S(1)} %bitcast.87, bf16[128,1024]{0,1:T(8,128)(2,1)S(1)} %bitcast.89, bf16[128,1024]{0,1:T(8,128)(2,1)S(1)} %bitcast.91), kind=kOutput, calls=%fused_computation.22 | convolution fusion | flops 807796736 | bytes 7340032 | tf_op jit(solution)/shard_map/dot_general | solution.py:77
  188.4 314.4 %all-reduce.3.cloned.1.call-done = f32[1024,3072]{0,1:T(8,128)} async-done(((f32[1024,3072]{0,1:T(8,128)}), f32[1024,3072]{0,1:T(8,128)}) %all-reduce.3.cloned.1.call-update) | async-done | bytes 12582928
  502.8 1.9 constant_dynamic-slice_fusion
  (32 shorter events, 16.4 us)
Async XLA Ops:
  7.2 1.2 copy-start
  7.2 88.1 %all-gather.7.cloned.1.call-start = ((), (), s32[]{:S(2)}) async-start(), calls=%async_computation.1 | async-start | bytes 17301504 | tf_op jit(solution)/shard_map/all_gather | solution.py:16
  13.4 161.5 %all-gather.5.cloned.1.call-start = ((), (), s32[]{:S(2)}) async-start(), calls=%async_computation | async-start | bytes 17301504 | tf_op jit(solution)/shard_map/all_gather | solution.py:16
  14.6 488.2 %all-reduce.3.cloned.1.call-start = ((), (), s32[]{:S(2)}) async-start(), calls=%async_computation.2 | async-start | bytes 25165824
Sparse Core Ops, SparseCore 0:
  13.5 81.7 all-gather.6
  97.9 77.0 all-gather.4
  182.8 319.9 all-reduce.2
where the time goes:
time: 515 us; the launch traced here: 512 us
  waiting for transfers between devices  437 us (85%)
  other arithmetic  36.3 us (7%)
  matrix products  20.1 us (4%)
  between operations  13.9 us (3%)
    unnamed x4, waiting for transfers between devices  314 us
    all_gather x2, waiting for transfers between devices, entering(): gathered = lax.all_gather(part, axis)  122 us
    add x31, other arithmetic, add_states(): return earlier + later  36.3 us
  transfers between devices with their start and end apart: 3, of which 3 were waited for; matrix products, arithmetic and copies ran while one was open for 9% of the time, Pallas kernels for 0%

commit v1 on v0

v1 whole, which is shorter than its diff:
```python
import functools
import math

import jax
import jax.numpy as jnp
from jax import lax
from jax.experimental import pallas as pl
from jax.experimental.pallas import tpu as pltpu
from jax.sharding import PartitionSpec as P

MESH = pl.DeviceIdType.MESH
F32 = jnp.float32
BF16 = jnp.bfloat16

HEADS = 8
HD = 128
ROWS = 128
WIDTH = 1024
INNER = HEADS * HD
NX, NY, NZ = 4, 4, 8
CHIPS = NX * NY
FLOWS = 6
FCOLS = 256
GROUPS = 128
STEPS = 7

ORDERS = (
    ("xu", "xv", "yu", "yv", "za", "zb", "zc"),
    ("xv", "xu", "yv", "yu", "zb", "za", "zc"),
    ("yu", "yv", "za", "zb", "xu", "xv", "zc"),
    ("yv", "yu", "zb", "za", "xv", "xu", "zc"),
    ("za", "zb", "xu", "xv", "yu", "yv", "zc"),
    ("zb", "za", "xv", "xu", "yv", "yu", "zc"),
)


def bits_of(x, y, z):
    return {
        "xu": (x % 2 + x // 2) % 2,
        "xv": x // 2,
        "yu": (y % 2 + y // 2) % 2,
        "yv": y // 2,
        "za": (z % 2 + (z // 2) % 2) % 2,
        "zb": (z // 2) % 2,
        "zc": z // 4,
    }


def place_of(flow, bits):
    total = 0
    for step, name in enumerate(ORDERS[flow]):
        total = total + bits[name] * (1 << (STEPS - 1 - step))
    return total


SHIFTS = sorted(
    ((dx, dy) for dx in range(NX) for dy in range(NY) if (dx, dy) != (0, 0)),
    key=lambda d: -(min(d[0], NX - d[0]) + min(d[1], NY - d[1])),
)


def dot(a, b, dims):
    return lax.dot_general(a, b, (dims, ((), ())), preferred_element_type=F32)


def kernel(
    scale,
    factor,
    tok_hbm,
    w_hbm,
    g_hbm,
    tg_ref,
    pg_ref,
    tok,
    g,
    w,
    proj,
    tokf,
    tokp,
    tokt,
    loc,
    s1b,
    tb,
    r1,
    eb,
    r2,
    s3b,
    lpart,
    st,
    qg,
    qf,
    qp,
    acc,
    rb,
    fin,
    finp,
    load_sem,
    pair_send,
    pair_recv,
    p1_send,
    p1_recv,
    p2_send,
    p2_recv,
    qp_send,
    qp_recv,
    rs_send,
    rs_recv,
):
    seq = lax.axis_index("seq")
    z = lax.axis_index("dp")
    core = seq % 2
    chip = seq // 2
    y = chip % NY
    x = chip // NY
    other = 1 - core

    def seq_at(cx, cy):
        return (cx * NY + cy) * 2 + core

    partner = (z, seq + 1 - 2 * core)
    near = {
        "xu": (z, seq_at(x + 1 - 2 * (x % 2), y)),
        "xv": (z, seq_at(3 - x, y)),
        "yu": (z, seq_at(x, y + 1 - 2 * (y % 2))),
        "yv": (z, seq_at(x, 3 - y)),
        "za": (z + 1 - 2 * (z % 2), seq),
        "zb": ((z + 2 * (z % 2) - 1 + NZ) % NZ, seq),
        "zc": ((z + 4) % NZ, seq),
    }
    bits = bits_of(x, y, z)
    targets = []
    for dx, dy in SHIFTS:
        tx, ty = (x + dx) % NX, (y + dy) % NY
        targets.append((tx * NY + ty, (z, seq_at(tx, ty))))

    def remote(src, dst, send, recv, device):
        return pltpu.make_async_remote_copy(
            src_ref=src,
            dst_ref=dst,
            send_sem=send,
            recv_sem=recv,
            device_id=device,
            device_id_type=MESH,
        )

    load_tok = pltpu.make_async_copy(tok_hbm, tok, load_sem.at[0])
    load_g = pltpu.make_async_copy(g_hbm, g, load_sem.at[1])
    load_tok.start()
    load_w = []
    for part in range(3):
        cols = pl.ds(part * INNER, INNER)
        load_w.append(
            pltpu.make_async_copy(w_hbm.at[:, cols], w.at[:, cols], load_sem.at[2 + part])
        )
        load_w[part].start()
    load_g.start()

    barrier = pltpu.get_barrier_semaphore()
    greeted = [partner, near["za"], near["zb"], near["zc"]] + [t[1] for t in targets]
    for device in greeted:
        pl.semaphore_signal(barrier, inc=1, device_id=device, device_id_type=MESH)

    load_tok.wait()
    tokf[...] = tok[...].astype(F32)
    pl.semaphore_wait(barrier, len(greeted))
    send_tok = remote(tokf, tokp, pair_send.at[0], pair_recv.at[0], partner)
    send_tok.start()

    for part in range(3):
        load_w[part].wait()

        def project(i, carry, part=part):
            cols = pl.ds(pl.multiple_of(part * INNER + i * 256, 256), 256)
            proj[:, cols] = dot(tok[...], w[:, cols], ((1,), (0,))).astype(BF16)
            return carry

        lax.fori_loop(0, INNER // 256, project, 0)
    load_g.wait()

    def head_cols(part, h):
        return pl.ds(pl.multiple_of(part * INNER + h * HD, HD), HD)

    def local_state(h, carry):
        q = proj[:, head_cols(0, h)]
        k = proj[:, head_cols(1, h)]
        v = proj[:, head_cols(2, h)]
        d = g[:, head_cols(0, h)]
        kv = dot(k, v, ((0,), (0,)))
        qd = scale * dot(q, d, ((0,), (0,)))
        loc[0, 2 * h] = kv[:64]
        loc[0, 2 * h + 1] = kv[64:]
        loc[1, 2 * h] = qd[:64]
        loc[1, 2 * h + 1] = qd[64:]
        return carry

    lax.fori_loop(0, HEADS, local_state, 0)

    pair_state = remote(loc.at[core], s1b, pair_send.at[1], pair_recv.at[1], partner)
    pair_state.start()

    def own_transpose(i, carry):
        rows = pl.ds(pl.multiple_of(i * 128, 128), 128)
        tokt[rows, 0:128] = tokf[:, rows].T.astype(BF16)
        return carry

    lax.fori_loop(0, WIDTH // 128, own_transpose, 0)

    pair_state.wait_recv()
    tb[...] = loc[other] + s1b[...]
    first = []
    for i, (target, device) in enumerate(targets):
        copy = remote(tb.at[target], r1.at[chip], p1_send.at[i], p1_recv.at[i], device)
        copy.start()
        first.append(copy)
    r1[chip] = tb[chip]

    row = lax.broadcasted_iota(jnp.int32, (ROWS, ROWS), 0)
    col = lax.broadcasted_iota(jnp.int32, (ROWS, ROWS), 1)
    causal = row >= col

    def inside(h, carry):
        q = proj[:, head_cols(0, h)]
        k = proj[:, head_cols(1, h)]
        v = proj[:, head_cols(2, h)]
        d = g[:, head_cols(0, h)]
        sa = jnp.where(causal, dot(d, v, ((1,), (1,))), 0.0).astype(BF16)
        sb = jnp.where(causal, dot(q, k, ((1,), (1,))), 0.0).astype(BF16)
        lpart[:, head_cols(0, h)] = dot(sa, k, ((1,), (0,)))
        lpart[:, head_cols(1, h)] = dot(sa, q, ((0,), (0,)))
        lpart[:, head_cols(2, h)] = dot(sb, d, ((0,), (0,)))
        return carry

    lax.fori_loop(0, HEADS, inside, 0)

    for copy in first:
        copy.wait_recv()

    running = jnp.zeros((64, HD), F32)
    for i in range(CHIPS):
        place = core * i + other * (CHIPS - 1 - i)
        eb[place] = running
        if i < CHIPS - 1:
            running = running + r1[place]
    second = []
    for i, (target, device) in enumerate(targets):
        copy = remote(eb.at[target], r2.at[chip], p2_send.at[i], p2_recv.at[i], device)
        copy.start()
        second.append(copy)
    r2[chip] = eb[chip]

    send_tok.wait_recv()

    def partner_transpose(i, carry):
        rows = pl.ds(pl.multiple_of(i * 128, 128), 128)
        tokt[rows, 128:256] = tokp[:, rows].T.astype(BF16)
        return carry

    lax.fori_loop(0, WIDTH // 128, partner_transpose, 0)

    for copy in second:
        copy.wait_recv()
    pair_scan = remote(r2, s3b, pair_send.at[2], pair_recv.at[2], partner)
    pair_scan.start()
    st[other] = (r2[...] + s1b[...]).astype(BF16)
    pair_scan.wait_recv()
    st[core] = s3b[...].astype(BF16)

    def finish(h):
        q_cols, k_cols, v_cols = (head_cols(part, h) for part in range(3))
        k = proj[:, k_cols]
        v = proj[:, v_cols]
        d = g[:, q_cols]
        prefix = jnp.concatenate([st[0, 2 * h], st[0, 2 * h + 1]], axis=0)
        suffix = jnp.concatenate([st[1, 2 * h], st[1, 2 * h + 1]], axis=0)
        dq = scale * (lpart[:, q_cols] + dot(d, prefix, ((1,), (1,))))
        dk = scale * lpart[:, k_cols] + dot(v, suffix, ((1,), (1,)))
        dv = scale * lpart[:, v_cols] + dot(k, suffix, ((1,), (0,)))
        out = [t.astype(BF16) for t in (dq, dk, dv)]
        for cols, t in zip((q_cols, k_cols, v_cols), out):
            qg[:, cols] = t
        return out

    gather = []
    for pair in range(2):
        for half in range(2):
            out = finish(other * 4 + 2 * pair + half)
            for part in range(3):
                qf[2 * part + pair, :, half * HD : (half + 1) * HD] = out[part].astype(F32)
        for part in range(3):
            flow = 2 * part + pair
            copy = remote(qf.at[flow], qp.at[flow], qp_send.at[flow], qp_recv.at[flow], partner)
            copy.start()
            gather.append((flow, copy))
    for i in range(4):
        finish(core * 4 + i)

    def halving(flow, step, base):
        size = GROUPS >> (step + 1)
        bit = bits[ORDERS[flow][step]]
        return remote(
            acc.at[flow, pl.ds(base + (1 - bit) * size, size)],
            rb.at[flow, pl.ds(size, size)],
            rs_send.at[flow, step],
            rs_recv.at[flow, step],
            near[ORDERS[flow][step]],
        )

    base = [0] * FLOWS
    steps = []
    current = [None] * FLOWS
    for flow, copy in gather:
        copy.wait_recv()
        part, pair = flow // 2, flow % 2
        cols = pl.ds(pl.multiple_of(part * INNER + core * 512 + pair * 256, 256), 256)
        rhs = jnp.concatenate([qg[:, cols], qp[flow].astype(BF16)], axis=0)

        def product(i, carry, flow=flow, rhs=rhs):
            rows = pl.ds(pl.multiple_of(i * 128, 128), 128)
            out = dot(tokt[rows, :], rhs, ((1,), (0,)))
            zero = bits_of(0, 0, i)
            start = place_of(flow, zero)
            for cx in range(NX):
                for cy in range(NY):
                    at = 8 * (cx * NY + cy)
                    acc[flow, start + place_of(flow, bits_of(cx, cy, 0))] = out[at : at + 8]
            return carry

        lax.fori_loop(0, NZ, product, 0)
        current[flow] = halving(flow, 0, 0)
        current[flow].start()
        steps.append(current[flow])

    def token_rows(i, carry):
        rows = pl.ds(pl.multiple_of(i * 256, 256), 256)
        tg_ref[:, rows] = dot(qg[...], w[rows, :], ((1,), (1,))).astype(BF16)
        return carry

    lax.fori_loop(0, WIDTH // 256, token_rows, 0)

    for step in range(STEPS):
        size = GROUPS >> (step + 1)
        for flow, _ in gather:
            current[flow].wait_recv()
            base[flow] = base[flow] + bits[ORDERS[flow][step]] * size
            kept = pl.ds(base[flow], size)
            acc[flow, kept] = acc[flow, kept] + rb[flow, size : 2 * size]
            if step + 1 < STEPS:
                current[flow] = halving(flow, step + 1, base[flow])
                current[flow].start()
                steps.append(current[flow])
            else:
                fin[flow] = acc[flow, base[flow]] * factor

    last = remote(fin, finp, pair_send.at[3], pair_recv.at[3], partner)
    last.start()
    low = core == 0
    for flow in range(FLOWS):
        part, pair = flow // 2, flow % 2
        mine = jnp.where(low, fin[flow, 0:4], fin[flow, 4:8])
        cols = pl.ds(pl.multiple_of(part * INNER + core * 512 + pair * 256, 256), 256)
        pg_ref[:, cols] = mine
    last.wait_recv()
    for flow in range(FLOWS):
        part, pair = flow // 2, flow % 2
        theirs = jnp.where(low, finp[flow, 0:4], finp[flow, 4:8])
        cols = pl.ds(pl.multiple_of(part * INNER + other * 512 + pair * 256, 256), 256)
        pg_ref[:, cols] = theirs

    for copy in [send_tok, pair_state, pair_scan, last] + first + second + steps:
        copy.wait_send()
    for _, copy in gather:
        copy.wait_send()


def shards(tokens, weights, dout):
    rows = tokens.shape[1]
    width = tokens.shape[2]
    seq_count = lax.axis_size("seq")
    data_count = lax.axis_size("dp")
    scale = 1.0 / math.sqrt(HD * rows * seq_count)
    factor = 1.0 / math.sqrt(data_count * rows * seq_count)
    any_space = pl.BlockSpec(memory_space=pl.ANY)
    vmem = pl.BlockSpec(memory_space=pltpu.VMEM)
    slices = (CHIPS, 64, HD)
    dma = pltpu.SemaphoreType.DMA
    token_grad, proj_grad = pl.pallas_call(
        functools.partial(kernel, scale, factor),
        out_shape=(
            jax.ShapeDtypeStruct((rows, width), BF16),
            jax.ShapeDtypeStruct((4, 3 * INNER), F32),
        ),
        in_specs=[any_space] * 3,
        out_specs=(vmem, vmem),
        scratch_shapes=[
            pltpu.VMEM((ROWS, WIDTH), BF16),
            pltpu.VMEM((ROWS, INNER), BF16),
            pltpu.VMEM((WIDTH, 3 * INNER), BF16),
            pltpu.VMEM((ROWS, 3 * INNER), BF16),
            pltpu.VMEM((ROWS, WIDTH), F32),
            pltpu.VMEM((ROWS, WIDTH), F32),
            pltpu.VMEM((WIDTH, 2 * ROWS), BF16),
            pltpu.VMEM((2,) + slices, F32),
            pltpu.VMEM(slices, F32),
            pltpu.VMEM(slices, F32),
            pltpu.VMEM(slices, F32),
            pltpu.VMEM(slices, F32),
            pltpu.VMEM(slices, F32),
            pltpu.VMEM(slices, F32),
            pltpu.VMEM((ROWS, 3 * INNER), F32),
            pltpu.VMEM((2,) + slices, BF16),
            pltpu.VMEM((ROWS, 3 * INNER), BF16),
            pltpu.VMEM((FLOWS, ROWS, FCOLS), F32),
            pltpu.VMEM((FLOWS, ROWS, FCOLS), F32),
            pltpu.VMEM((FLOWS, GROUPS, 8, FCOLS), F32),
            pltpu.VMEM((FLOWS, GROUPS, 8, FCOLS), F32),
            pltpu.VMEM((FLOWS, 8, FCOLS), F32),
            pltpu.VMEM((FLOWS, 8, FCOLS), F32),
            dma((5,)),
            dma((4,)),
            dma((4,)),
            dma((CHIPS - 1,)),
            dma((CHIPS - 1,)),
            dma((CHIPS - 1,)),
            dma((CHIPS - 1,)),
            dma((FLOWS,)),
            dma((FLOWS,)),
            dma((FLOWS, STEPS)),
            dma((FLOWS, STEPS)),
        ],
        compiler_params=pltpu.CompilerParams(
            collective_id=0, has_side_effects=True, vmem_limit_bytes=60 * 1024 * 1024
        ),
    )(tokens.reshape(rows, width), weights, dout.reshape(rows, INNER))
    return (token_grad.reshape(1, rows, width), proj_grad)


def solution(mesh):
    in_specs = (P("dp", "seq", None), P(), P("dp", "seq", None))
    out_specs = (P("dp", "seq", None), P(("dp", "seq"), None))
    return jax.shard_map(shards, mesh=mesh, in_specs=in_specs, out_specs=out_specs, check_vma=False)
```

time: 515 us -> 92 us (0.18)
  waiting for transfers between devices: 437 us -> 0 us
  Pallas kernels: 0 us -> 88.1 us
  other arithmetic: 36.3 us -> 0 us
  matrix products: 20.1 us -> 0 us
  between operations: 13.9 us -> 0.64 us
    unnamed x4 -> x0, waiting for transfers between devices: 314 us -> none
    all_gather x2 -> x0, waiting for transfers between devices: 122 us -> none  [entering(): gathered = lax.all_gather(part, axis)]
    pallas_call x0 -> x1, Pallas kernels: none -> 88.1 us  [shards(): pl.pallas_call(functools.partial(kernel, scale, factor), out_shape=(jax.S...]
    add x31 -> x0, other arithmetic: 36.3 us -> none  [add_states(): return earlier + later]
    dot_general x12 -> x0, matrix products: 20.1 us -> none  [the longest x1 6.26 us: shards(): lax.dot_general(flat, qkv_grad, (((0,), (0,)), ((), ())), preferred_eleme...]
  transfers between devices with their start and end apart: 3 -> 0, of which waited for: 3 -> 0; matrix products, arithmetic and copies ran while one was open for 9% -> 0% of each run, Pallas kernels for 0% -> 0%
where the time goes in v1:
time: 92 us; the launch traced here: 91.9 us
  Pallas kernels  88.1 us (96%)
  local copies, waits for them, and re-layouts  3.09 us (3%)
    pallas_call x1, Pallas kernels, shards(): pl.pallas_call(functools.partial(kernel, scale, factor), out_shape=(jax.S...  88.1 us
    unnamed x2, local copies, waits for them, and re-layouts  3.09 us

profile of v1, /device:TPU:1, one launch (start us, length us, event | category | flops | bytes accessed | tf_op | source)
XLA Modules:
  0.0 91.9 jit_solution(11069870673184524019)
XLA Ops:
  0.6 88.1 %shard_map.50 = (bf16[128,1024]{1,0:T(8,128)(2,1)}, f32[4,3072]{1,0:T(4,128)}) custom-call(bf16[128,1024]{1,0:T(8,128)(2,1)} %bitcast.4, bf16[1024,3072]{1,0:T(8,128)(2,1)} %w_hbm.1, bf16[128,1024]{1,0:T(8,128)(2,1)} %bitcast.5), custom_call_target="tpu_custom_call" | custom-call | tf_op jit(solution)/shard_map/pallas_call | solution.py:386
  88.8 1.7 %copy.7 = bf16[1,128,1024]{2,1,0:T(8,128)(2,1)} copy(bf16[1,128,1024]{2,1,0:T(8,128)(2,1)} %bitcast.3) | data formatting | bytes 524288
  90.4 1.4 %copy.8 = f32[4,3072]{1,0:T(4,128)} copy(f32[4,3072]{1,0:T(4,128)} %get-tuple-element.9) | data formatting | bytes 98304

commit v2 on v1

--- a/solution.py
+++ b/solution.py
@@ -20,17 +20,16 @@
 NX, NY, NZ = 4, 4, 8
 CHIPS = NX * NY
 FLOWS = 6
-FCOLS = 256
 GROUPS = 128
-STEPS = 7
+STEPS = 6
 
 ORDERS = (
     ("xu", "xv", "yu", "yv", "za", "zb", "zc"),
     ("xv", "xu", "yv", "yu", "zb", "za", "zc"),
     ("yu", "yv", "za", "zb", "xu", "xv", "zc"),
     ("yv", "yu", "zb", "za", "xv", "xu", "zc"),
+    ("zb", "za", "xv", "xu", "yv", "yu", "zc"),
     ("za", "zb", "xu", "xv", "yu", "yv", "zc"),
-    ("zb", "za", "xv", "xu", "yv", "yu", "zc"),
 )
 
 
@@ -47,9 +46,9 @@
 
 
 def place_of(flow, bits):
-    total = 0
-    for step, name in enumerate(ORDERS[flow]):
-        total = total + bits[name] * (1 << (STEPS - 1 - step))
+    total = bits[ORDERS[flow][0]]
+    for step, name in enumerate(ORDERS[flow][1:]):
+        total = total + bits[name] * (GROUPS >> (step + 1))
     return total
 
 
@@ -76,8 +75,10 @@
     w,
     proj,
     tokf,
-    tokp,
+    tkr,
+    tkx,
     tokt,
+    tokx,
     loc,
     s1b,
     tb,
@@ -89,22 +90,26 @@
     st,
     qg,
     qf,
-    qp,
+    qr,
     acc,
     rb,
     fin,
-    finp,
+    fr,
     load_sem,
     pair_send,
     pair_recv,
+    tk_send,
+    tk_recv,
     p1_send,
     p1_recv,
     p2_send,
     p2_recv,
-    qp_send,
-    qp_recv,
+    q_send,
+    q_recv,
     rs_send,
     rs_recv,
+    f_send,
+    f_recv,
 ):
     seq = lax.axis_index("seq")
     z = lax.axis_index("dp")
@@ -127,6 +132,11 @@
         "zb": ((z + 2 * (z % 2) - 1 + NZ) % NZ, seq),
         "zc": ((z + 4) % NZ, seq),
     }
+    home = dict(near, zb=((z // 4) * 4 + 3 - z % 4, seq))
+
+    def crossed(device):
+        return (device[0], device[1] + 1 - 2 * core)
+
     bits = bits_of(x, y, z)
     targets = []
     for dx, dy in SHIFTS:
@@ -157,13 +167,29 @@
 
     barrier = pltpu.get_barrier_semaphore()
     greeted = [partner, near["za"], near["zb"], near["zc"]] + [t[1] for t in targets]
+    greeted += [crossed(near[order[0]]) for order in ORDERS]
+    greeted += [home["zb"], crossed(home["zb"])]
     for device in greeted:
         pl.semaphore_signal(barrier, inc=1, device_id=device, device_id_type=MESH)
 
     load_tok.wait()
-    tokf[...] = tok[...].astype(F32)
+
+    def own_transpose(i, carry):
+        rows = pl.ds(pl.multiple_of(i * 128, 128), 128)
+        flipped = tok[:, rows].astype(F32).T
+        tokf[rows, :] = flipped
+        tokt[rows, 0:128] = flipped.astype(BF16)
+        return carry
+
+    lax.fori_loop(0, WIDTH // 128, own_transpose, 0)
     pl.semaphore_wait(barrier, len(greeted))
-    send_tok = remote(tokf, tokp, pair_send.at[0], pair_recv.at[0], partner)
+    tokens_out = []
+    for flow in range(FLOWS):
+        link = near[ORDERS[flow][0]]
+        copy = remote(tokf, tkr.at[flow], tk_send.at[flow], tk_recv.at[flow], link)
+        copy.start()
+        tokens_out.append(copy)
+    send_tok = remote(tokf, tkr.at[FLOWS], pair_send.at[0], pair_recv.at[0], partner)
     send_tok.start()
 
     for part in range(3):
@@ -198,13 +224,6 @@
     pair_state = remote(loc.at[core], s1b, pair_send.at[1], pair_recv.at[1], partner)
     pair_state.start()
 
-    def own_transpose(i, carry):
-        rows = pl.ds(pl.multiple_of(i * 128, 128), 128)
-        tokt[rows, 0:128] = tokf[:, rows].T.astype(BF16)
-        return carry
-
-    lax.fori_loop(0, WIDTH // 128, own_transpose, 0)
-
     pair_state.wait_recv()
     tb[...] = loc[other] + s1b[...]
     first = []
@@ -231,6 +250,15 @@
         return carry
 
     lax.fori_loop(0, HEADS, inside, 0)
+
+    relays = []
+    for flow in range(FLOWS):
+        tokens_out[flow].wait_recv()
+        copy = remote(
+            tkr.at[flow], tkx.at[flow], tk_send.at[FLOWS + flow], tk_recv.at[FLOWS + flow], partner
+        )
+        copy.start()
+        relays.append(copy)
 
     for copy in first:
         copy.wait_recv()
@@ -249,13 +277,11 @@
     r2[chip] = eb[chip]
 
     send_tok.wait_recv()
-
-    def partner_transpose(i, carry):
-        rows = pl.ds(pl.multiple_of(i * 128, 128), 128)
-        tokt[rows, 128:256] = tokp[:, rows].T.astype(BF16)
-        return carry
-
-    lax.fori_loop(0, WIDTH // 128, partner_transpose, 0)
+    tokt[:, 128:256] = tkr[FLOWS].astype(BF16)
+    for flow in range(FLOWS):
+        tokx[flow, :, 0:128] = tkr[flow].astype(BF16)
+        relays[flow].wait_recv()
+        tokx[flow, :, 128:256] = tkx[flow].astype(BF16)
 
     for copy in second:
         copy.wait_recv()
@@ -276,53 +302,95 @@
         dk = scale * lpart[:, k_cols] + dot(v, suffix, ((1,), (1,)))
         dv = scale * lpart[:, v_cols] + dot(k, suffix, ((1,), (0,)))
         out = [t.astype(BF16) for t in (dq, dk, dv)]
-        for cols, t in zip((q_cols, k_cols, v_cols), out):
+        for part, (cols, t) in enumerate(zip((q_cols, k_cols, v_cols), out)):
             qg[:, cols] = t
-        return out
-
-    gather = []
+            qf[part, h] = t.astype(F32)
+
+    first_bit = [bits[ORDERS[flow][0]] for flow in range(FLOWS)]
+
+    def head_of(flow, at_core, bit):
+        return 4 * at_core + 2 * (flow % 2) + bit
+
+    gather = [None] * FLOWS
     for pair in range(2):
-        for half in range(2):
-            out = finish(other * 4 + 2 * pair + half)
-            for part in range(3):
-                qf[2 * part + pair, :, half * HD : (half + 1) * HD] = out[part].astype(F32)
-        for part in range(3):
+        for h in (0, 1, 4, 5):
+            finish(2 * pair + h)
+        for part in (2, 1, 0):
             flow = 2 * part + pair
-            copy = remote(qf.at[flow], qp.at[flow], qp_send.at[flow], qp_recv.at[flow], partner)
-            copy.start()
-            gather.append((flow, copy))
-    for i in range(4):
-        finish(core * 4 + i)
+            bit = first_bit[flow]
+            link = ORDERS[flow][0]
+            copies = []
+            for i, (at_core, at_bit, device) in enumerate(
+                (
+                    (core, 1 - bit, near[link]),
+                    (other, 1 - bit, crossed(near[link])),
+                    (other, bit, partner),
+                )
+            ):
+                copy = remote(
+                    qf.at[part, head_of(flow, at_core, at_bit)],
+                    qr.at[flow, i],
+                    q_send.at[flow, i],
+                    q_recv.at[flow, i],
+                    device,
+                )
+                copy.start()
+                copies.append(copy)
+            gather[flow] = copies
+
+    for part in range(3):
+        blocks = []
+        for pair in range(2):
+            flow = 2 * part + pair
+            gather[flow][2].wait_recv()
+            own = qg[:, head_cols(part, head_of(flow, core, first_bit[flow]))]
+            blocks.append(jnp.concatenate([own, qr[flow, 2].astype(BF16)], axis=0))
+        rhs = jnp.concatenate(blocks, axis=1)
+
+        def chip_product(i, carry, part=part, rhs=rhs):
+            rows = pl.ds(pl.multiple_of(i * 128, 128), 128)
+            out = dot(tokt[rows, :], rhs, ((1,), (0,)))
+            for pair in range(2):
+                flow = 2 * part + pair
+                start = place_of(flow, bits_of(0, 0, i))
+                for cx in range(NX):
+                    for cy in range(NY):
+                        at = 8 * (cx * NY + cy)
+                        block = out[at : at + 8, pair * 128 : pair * 128 + 128]
+                        acc[flow, start + place_of(flow, bits_of(cx, cy, 0))] = block
+            return carry
+
+        lax.fori_loop(0, NZ, chip_product, 0)
 
     def halving(flow, step, base):
         size = GROUPS >> (step + 1)
-        bit = bits[ORDERS[flow][step]]
+        name = ORDERS[flow][step + 1]
         return remote(
-            acc.at[flow, pl.ds(base + (1 - bit) * size, size)],
+            acc.at[flow, pl.ds(base + (1 - bits[name]) * size, size)],
             rb.at[flow, pl.ds(size, size)],
             rs_send.at[flow, step],
             rs_recv.at[flow, step],
-            near[ORDERS[flow][step]],
+            near[name],
         )
 
     base = [0] * FLOWS
     steps = []
     current = [None] * FLOWS
-    for flow, copy in gather:
-        copy.wait_recv()
-        part, pair = flow // 2, flow % 2
-        cols = pl.ds(pl.multiple_of(part * INNER + core * 512 + pair * 256, 256), 256)
-        rhs = jnp.concatenate([qg[:, cols], qp[flow].astype(BF16)], axis=0)
+    flow_order = (4, 2, 0, 5, 3, 1)
+    for flow in flow_order:
+        gather[flow][0].wait_recv()
+        gather[flow][1].wait_recv()
+        rhs = jnp.concatenate([qr[flow, 0].astype(BF16), qr[flow, 1].astype(BF16)], axis=0)
 
         def product(i, carry, flow=flow, rhs=rhs):
             rows = pl.ds(pl.multiple_of(i * 128, 128), 128)
-            out = dot(tokt[rows, :], rhs, ((1,), (0,)))
-            zero = bits_of(0, 0, i)
-            start = place_of(flow, zero)
+            out = dot(tokx[flow, rows, :], rhs, ((1,), (0,)))
+            start = place_of(flow, bits_of(0, 0, i))
             for cx in range(NX):
                 for cy in range(NY):
                     at = 8 * (cx * NY + cy)
-                    acc[flow, start + place_of(flow, bits_of(cx, cy, 0))] = out[at : at + 8]
+                    place = start + place_of(flow, bits_of(cx, cy, 0))
+                    acc[flow, place] = acc[flow, place] + out[at : at + 8]
             return carry
 
         lax.fori_loop(0, NZ, product, 0)
@@ -337,11 +405,26 @@
 
     lax.fori_loop(0, WIDTH // 256, token_rows, 0)
 
+    def hand_out(flow):
+        bit = first_bit[flow]
+        device = home[ORDERS[flow][0]]
+        fin[flow, 0] = acc[flow, base[flow] + bit] * factor
+        fin[flow, 1] = acc[flow, base[flow] + 1 - bit] * factor
+        copies = []
+        for i, (src, to) in enumerate(((1, device), (1, crossed(device)), (0, partner))):
+            copy = remote(
+                fin.at[flow, src], fr.at[flow, i], f_send.at[flow, i], f_recv.at[flow, i], to
+            )
+            copy.start()
+            copies.append(copy)
+        return copies
+
+    handed = [None] * FLOWS
     for step in range(STEPS):
         size = GROUPS >> (step + 1)
-        for flow, _ in gather:
+        for flow in flow_order:
             current[flow].wait_recv()
-            base[flow] = base[flow] + bits[ORDERS[flow][step]] * size
+            base[flow] = base[flow] + bits[ORDERS[flow][step + 1]] * size
             kept = pl.ds(base[flow], size)
             acc[flow, kept] = acc[flow, kept] + rb[flow, size : 2 * size]
             if step + 1 < STEPS:
@@ -349,27 +432,29 @@
                 current[flow].start()
                 steps.append(current[flow])
             else:
-                fin[flow] = acc[flow, base[flow]] * factor
-
-    last = remote(fin, finp, pair_send.at[3], pair_recv.at[3], partner)
-    last.start()
+                handed[flow] = hand_out(flow)
+
     low = core == 0
+
+    def put(flow, at_core, bit, rows):
+        cols = head_cols(flow // 2, head_of(flow, at_core, bit))
+        pg_ref[:, cols] = jnp.where(low, rows[0:4], rows[4:8])
+
+    for flow in flow_order:
+        put(flow, core, first_bit[flow], fin[flow, 0])
+    for flow in flow_order:
+        bit = first_bit[flow]
+        for copy in handed[flow]:
+            copy.wait_recv()
+        put(flow, core, 1 - bit, fr[flow, 0])
+        put(flow, other, 1 - bit, fr[flow, 1])
+        put(flow, other, bit, fr[flow, 2])
+
+    for copy in [send_tok, pair_state, pair_scan] + tokens_out + relays + first + second + steps:
+        copy.wait_send()
     for flow in range(FLOWS):
-        part, pair = flow // 2, flow % 2
-        mine = jnp.where(low, fin[flow, 0:4], fin[flow, 4:8])
-        cols = pl.ds(pl.multiple_of(part * INNER + core * 512 + pair * 256, 256), 256)
-        pg_ref[:, cols] = mine
-    last.wait_recv()
-    for flow in range(FLOWS):
-        part, pair = flow // 2, flow % 2
-        theirs = jnp.where(low, finp[flow, 0:4], finp[flow, 4:8])
-        cols = pl.ds(pl.multiple_of(part * INNER + other * 512 + pair * 256, 256), 256)
-        pg_ref[:, cols] = theirs
-
-    for copy in [send_tok, pair_state, pair_scan, last] + first + second + steps:
-        copy.wait_send()
-    for _, copy in gather:
-        copy.wait_send()
+        for copy in gather[flow] + handed[flow]:
+            copy.wait_send()
 
 
 def shards(tokens, weights, dout):
@@ -396,9 +481,11 @@
             pltpu.VMEM((ROWS, INNER), BF16),
             pltpu.VMEM((WIDTH, 3 * INNER), BF16),
             pltpu.VMEM((ROWS, 3 * INNER), BF16),
-            pltpu.VMEM((ROWS, WIDTH), F32),
-            pltpu.VMEM((ROWS, WIDTH), F32),
+            pltpu.VMEM((WIDTH, ROWS), F32),
+            pltpu.VMEM((FLOWS + 1, WIDTH, ROWS), F32),
+            pltpu.VMEM((FLOWS, WIDTH, ROWS), F32),
             pltpu.VMEM((WIDTH, 2 * ROWS), BF16),
+            pltpu.VMEM((FLOWS, WIDTH, 2 * ROWS), BF16),
             pltpu.VMEM((2,) + slices, F32),
             pltpu.VMEM(slices, F32),
             pltpu.VMEM(slices, F32),
@@ -409,23 +496,27 @@
             pltpu.VMEM((ROWS, 3 * INNER), F32),
             pltpu.VMEM((2,) + slices, BF16),
             pltpu.VMEM((ROWS, 3 * INNER), BF16),
-            pltpu.VMEM((FLOWS, ROWS, FCOLS), F32),
-            pltpu.VMEM((FLOWS, ROWS, FCOLS), F32),
-            pltpu.VMEM((FLOWS, GROUPS, 8, FCOLS), F32),
-            pltpu.VMEM((FLOWS, GROUPS, 8, FCOLS), F32),
-            pltpu.VMEM((FLOWS, 8, FCOLS), F32),
-            pltpu.VMEM((FLOWS, 8, FCOLS), F32),
+            pltpu.VMEM((3, HEADS, ROWS, HD), F32),
+            pltpu.VMEM((FLOWS, 3, ROWS, HD), F32),
+            pltpu.VMEM((FLOWS, GROUPS, 8, HD), F32),
+            pltpu.VMEM((FLOWS, GROUPS, 8, HD), F32),
+            pltpu.VMEM((FLOWS, 2, 8, HD), F32),
+            pltpu.VMEM((FLOWS, 3, 8, HD), F32),
             dma((5,)),
-            dma((4,)),
-            dma((4,)),
+            dma((3,)),
+            dma((3,)),
+            dma((2 * FLOWS,)),
+            dma((2 * FLOWS,)),
             dma((CHIPS - 1,)),
             dma((CHIPS - 1,)),
             dma((CHIPS - 1,)),
             dma((CHIPS - 1,)),
-            dma((FLOWS,)),
-            dma((FLOWS,)),
+            dma((FLOWS, 3)),
+            dma((FLOWS, 3)),
             dma((FLOWS, STEPS)),
             dma((FLOWS, STEPS)),
+            dma((FLOWS, 3)),
+            dma((FLOWS, 3)),
         ],
         compiler_params=pltpu.CompilerParams(
             collective_id=0, has_side_effects=True, vmem_limit_bytes=60 * 1024 * 1024

time: 92 us -> 88.5 us (0.962)
  Pallas kernels: 88.1 us -> 84.7 us
    pallas_call x1, Pallas kernels: 88.1 us -> 84.7 us  [shards(): pl.pallas_call(functools.partial(kernel, scale, factor), out_shape=(jax.S...]
where the time goes in v2:
time: 88.5 us; the launch traced here: 88.4 us
  Pallas kernels  84.7 us (96%)
  local copies, waits for them, and re-layouts  3.09 us (3%)
    pallas_call x1, Pallas kernels, shards(): pl.pallas_call(functools.partial(kernel, scale, factor), out_shape=(jax.S...  84.7 us
    unnamed x2, local copies, waits for them, and re-layouts  3.09 us

profile of v2, /device:TPU:1, one launch (start us, length us, event | category | flops | bytes accessed | tf_op | source)
XLA Modules:
  0.0 88.4 jit_solution(2879383008945505079)
XLA Ops:
  0.6 84.7 %shard_map.50 = (bf16[128,1024]{1,0:T(8,128)(2,1)}, f32[4,3072]{1,0:T(4,128)}) custom-call(bf16[128,1024]{1,0:T(8,128)(2,1)} %bitcast.4, bf16[1024,3072]{1,0:T(8,128)(2,1)} %w_hbm.1, bf16[128,1024]{1,0:T(8,128)(2,1)} %bitcast.5), custom_call_target="tpu_custom_call" | custom-call | tf_op jit(solution)/shard_map/pallas_call | solution.py:471
  85.3 1.7 %copy.7 = bf16[1,128,1024]{2,1,0:T(8,128)(2,1)} copy(bf16[1,128,1024]{2,1,0:T(8,128)(2,1)} %bitcast.3) | data formatting | bytes 524288
  87.0 1.4 %copy.8 = f32[4,3072]{1,0:T(4,128)} copy(f32[4,3072]{1,0:T(4,128)} %get-tuple-element.9) | data formatting | bytes 98304

commit v3 on v2

--- a/solution.py
+++ b/solution.py
@@ -19,6 +19,8 @@
 INNER = HEADS * HD
 NX, NY, NZ = 4, 4, 8
 CHIPS = NX * NY
+CHUNKS = 2
+SLICE = 32
 FLOWS = 6
 GROUPS = 128
 STEPS = 6
@@ -78,7 +80,6 @@
     tkr,
     tkx,
     tokt,
-    tokx,
     loc,
     s1b,
     tb,
@@ -182,15 +183,6 @@
         return carry
 
     lax.fori_loop(0, WIDTH // 128, own_transpose, 0)
-    pl.semaphore_wait(barrier, len(greeted))
-    tokens_out = []
-    for flow in range(FLOWS):
-        link = near[ORDERS[flow][0]]
-        copy = remote(tokf, tkr.at[flow], tk_send.at[flow], tk_recv.at[flow], link)
-        copy.start()
-        tokens_out.append(copy)
-    send_tok = remote(tokf, tkr.at[FLOWS], pair_send.at[0], pair_recv.at[0], partner)
-    send_tok.start()
 
     for part in range(3):
         load_w[part].wait()
@@ -206,32 +198,86 @@
     def head_cols(part, h):
         return pl.ds(pl.multiple_of(part * INNER + h * HD, HD), HD)
 
-    def local_state(h, carry):
-        q = proj[:, head_cols(0, h)]
-        k = proj[:, head_cols(1, h)]
-        v = proj[:, head_cols(2, h)]
-        d = g[:, head_cols(0, h)]
-        kv = dot(k, v, ((0,), (0,)))
-        qd = scale * dot(q, d, ((0,), (0,)))
-        loc[0, 2 * h] = kv[:64]
-        loc[0, 2 * h + 1] = kv[64:]
-        loc[1, 2 * h] = qd[:64]
-        loc[1, 2 * h + 1] = qd[64:]
-        return carry
-
-    lax.fori_loop(0, HEADS, local_state, 0)
-
-    pair_state = remote(loc.at[core], s1b, pair_send.at[1], pair_recv.at[1], partner)
-    pair_state.start()
-
-    pair_state.wait_recv()
-    tb[...] = loc[other] + s1b[...]
+    pl.semaphore_wait(barrier, len(greeted))
+    half = WIDTH // 2
+    tokens_out = {}
+    relays = {}
+
+    def send_tokens(flows, part):
+        rows = pl.ds(part * half, half)
+        for flow in flows:
+            copy = remote(
+                tokf.at[rows],
+                tkr.at[flow, rows],
+                tk_send.at[flow, part],
+                tk_recv.at[flow, part],
+                near[ORDERS[flow][0]],
+            )
+            copy.start()
+            tokens_out[flow, part] = copy
+
+    def relay_tokens(flows, part):
+        rows = pl.ds(part * half, half)
+        for flow in flows:
+            tokens_out[flow, part].wait_recv()
+            copy = remote(
+                tkr.at[flow, rows],
+                tkx.at[flow, rows],
+                tk_send.at[FLOWS + flow, part],
+                tk_recv.at[FLOWS + flow, part],
+                partner,
+            )
+            copy.start()
+            relays[flow, part] = copy
+
+    z_flows, xy_flows = (4, 5), (0, 1, 2, 3)
+    send_tokens(z_flows, 0)
+    send_tokens(z_flows, 1)
+
+    pair_state = []
+    for chunk in range(CHUNKS):
+
+        def local_state(i, carry, chunk=chunk):
+            h = 4 * chunk + i
+            q = proj[:, head_cols(0, h)]
+            k = proj[:, head_cols(1, h)]
+            v = proj[:, head_cols(2, h)]
+            d = g[:, head_cols(0, h)]
+            loc[0, chunk, pl.ds(4 * i, 4)] = dot(k, v, ((0,), (0,))).reshape(4, SLICE, HD)
+            loc[1, chunk, pl.ds(4 * i, 4)] = (scale * dot(q, d, ((0,), (0,)))).reshape(4, SLICE, HD)
+            return carry
+
+        lax.fori_loop(0, HEADS // CHUNKS, local_state, 0)
+        copy = remote(
+            loc.at[core, chunk],
+            s1b.at[chunk],
+            pair_send.at[chunk],
+            pair_recv.at[chunk],
+            partner,
+        )
+        copy.start()
+        pair_state.append(copy)
+
     first = []
-    for i, (target, device) in enumerate(targets):
-        copy = remote(tb.at[target], r1.at[chip], p1_send.at[i], p1_recv.at[i], device)
-        copy.start()
-        first.append(copy)
-    r1[chip] = tb[chip]
+    for chunk in range(CHUNKS):
+        pair_state[chunk].wait_recv()
+        tb[chunk] = loc[other, chunk] + s1b[chunk]
+        copies = []
+        for i, (target, device) in enumerate(targets):
+            copy = remote(
+                tb.at[chunk, target],
+                r1.at[chunk, chip],
+                p1_send.at[chunk, i],
+                p1_recv.at[chunk, i],
+                device,
+            )
+            copy.start()
+            copies.append(copy)
+        first.append(copies)
+        r1[chunk, chip] = tb[chunk, chip]
+    send_tokens(xy_flows, 0)
+    send_tok = remote(tokf, tkr.at[FLOWS], pair_send.at[4], pair_recv.at[4], partner)
+    send_tok.start()
 
     row = lax.broadcasted_iota(jnp.int32, (ROWS, ROWS), 0)
     col = lax.broadcasted_iota(jnp.int32, (ROWS, ROWS), 1)
@@ -251,53 +297,60 @@
 
     lax.fori_loop(0, HEADS, inside, 0)
 
-    relays = []
-    for flow in range(FLOWS):
-        tokens_out[flow].wait_recv()
+    second = []
+    for chunk in range(CHUNKS):
+        for copy in first[chunk]:
+            copy.wait_recv()
+        running = jnp.zeros((SLICE, HD), F32)
+        for i in range(CHIPS):
+            place = core * i + other * (CHIPS - 1 - i)
+            eb[chunk, place] = running
+            if i < CHIPS - 1:
+                running = running + r1[chunk, place]
+        copies = []
+        for i, (target, device) in enumerate(targets):
+            copy = remote(
+                eb.at[chunk, target],
+                r2.at[chunk, chip],
+                p2_send.at[chunk, i],
+                p2_recv.at[chunk, i],
+                device,
+            )
+            copy.start()
+            copies.append(copy)
+        second.append(copies)
+        r2[chunk, chip] = eb[chunk, chip]
+
+    send_tokens(xy_flows, 1)
+    relay_tokens(z_flows, 0)
+    relay_tokens(z_flows, 1)
+    relay_tokens(xy_flows, 0)
+    send_tok.wait_recv()
+    tokt[:, 128:256] = tkr[FLOWS].astype(BF16)
+
+    pair_scan = []
+    for chunk in range(CHUNKS):
+        for copy in second[chunk]:
+            copy.wait_recv()
         copy = remote(
-            tkr.at[flow], tkx.at[flow], tk_send.at[FLOWS + flow], tk_recv.at[FLOWS + flow], partner
+            r2.at[chunk],
+            s3b.at[chunk],
+            pair_send.at[2 + chunk],
+            pair_recv.at[2 + chunk],
+            partner,
         )
         copy.start()
-        relays.append(copy)
-
-    for copy in first:
-        copy.wait_recv()
-
-    running = jnp.zeros((64, HD), F32)
-    for i in range(CHIPS):
-        place = core * i + other * (CHIPS - 1 - i)
-        eb[place] = running
-        if i < CHIPS - 1:
-            running = running + r1[place]
-    second = []
-    for i, (target, device) in enumerate(targets):
-        copy = remote(eb.at[target], r2.at[chip], p2_send.at[i], p2_recv.at[i], device)
-        copy.start()
-        second.append(copy)
-    r2[chip] = eb[chip]
-
-    send_tok.wait_recv()
-    tokt[:, 128:256] = tkr[FLOWS].astype(BF16)
-    for flow in range(FLOWS):
-        tokx[flow, :, 0:128] = tkr[flow].astype(BF16)
-        relays[flow].wait_recv()
-        tokx[flow, :, 128:256] = tkx[flow].astype(BF16)
-
-    for copy in second:
-        copy.wait_recv()
-    pair_scan = remote(r2, s3b, pair_send.at[2], pair_recv.at[2], partner)
-    pair_scan.start()
-    st[other] = (r2[...] + s1b[...]).astype(BF16)
-    pair_scan.wait_recv()
-    st[core] = s3b[...].astype(BF16)
+        pair_scan.append(copy)
+        st[other, chunk] = (r2[chunk] + s1b[chunk]).astype(BF16)
 
     def finish(h):
         q_cols, k_cols, v_cols = (head_cols(part, h) for part in range(3))
         k = proj[:, k_cols]
         v = proj[:, v_cols]
         d = g[:, q_cols]
-        prefix = jnp.concatenate([st[0, 2 * h], st[0, 2 * h + 1]], axis=0)
-        suffix = jnp.concatenate([st[1, 2 * h], st[1, 2 * h + 1]], axis=0)
+        at = 4 * (h % 4)
+        prefix = st[0, h // 4, at : at + 4].reshape(HD, HD)
+        suffix = st[1, h // 4, at : at + 4].reshape(HD, HD)
         dq = scale * (lpart[:, q_cols] + dot(d, prefix, ((1,), (1,))))
         dk = scale * lpart[:, k_cols] + dot(v, suffix, ((1,), (1,)))
         dv = scale * lpart[:, v_cols] + dot(k, suffix, ((1,), (0,)))
@@ -309,12 +362,14 @@
     first_bit = [bits[ORDERS[flow][0]] for flow in range(FLOWS)]
 
     def head_of(flow, at_core, bit):
-        return 4 * at_core + 2 * (flow % 2) + bit
+        return 4 * (flow % 2) + 2 * at_core + bit
 
     gather = [None] * FLOWS
     for pair in range(2):
-        for h in (0, 1, 4, 5):
-            finish(2 * pair + h)
+        pair_scan[pair].wait_recv()
+        st[core, pair] = s3b[pair].astype(BF16)
+        for h in range(4):
+            finish(4 * pair + h)
         for part in (2, 1, 0):
             flow = 2 * part + pair
             bit = first_bit[flow]
@@ -338,25 +393,27 @@
                 copies.append(copy)
             gather[flow] = copies
 
-    for part in range(3):
+    relay_tokens(xy_flows, 1)
+
+    def chip_part(pair):
         blocks = []
-        for pair in range(2):
+        for part in range(3):
             flow = 2 * part + pair
             gather[flow][2].wait_recv()
             own = qg[:, head_cols(part, head_of(flow, core, first_bit[flow]))]
             blocks.append(jnp.concatenate([own, qr[flow, 2].astype(BF16)], axis=0))
         rhs = jnp.concatenate(blocks, axis=1)
 
-        def chip_product(i, carry, part=part, rhs=rhs):
+        def chip_product(i, carry):
             rows = pl.ds(pl.multiple_of(i * 128, 128), 128)
             out = dot(tokt[rows, :], rhs, ((1,), (0,)))
-            for pair in range(2):
+            for part in range(3):
                 flow = 2 * part + pair
                 start = place_of(flow, bits_of(0, 0, i))
                 for cx in range(NX):
                     for cy in range(NY):
                         at = 8 * (cx * NY + cy)
-                        block = out[at : at + 8, pair * 128 : pair * 128 + 128]
+                        block = out[at : at + 8, part * 128 : part * 128 + 128]
                         acc[flow, start + place_of(flow, bits_of(cx, cy, 0))] = block
             return carry
 
@@ -378,13 +435,20 @@
     current = [None] * FLOWS
     flow_order = (4, 2, 0, 5, 3, 1)
     for flow in flow_order:
+        if flow in (4, 5):
+            chip_part(flow % 2)
+        relays[flow, 0].wait_recv()
+        relays[flow, 1].wait_recv()
         gather[flow][0].wait_recv()
         gather[flow][1].wait_recv()
         rhs = jnp.concatenate([qr[flow, 0].astype(BF16), qr[flow, 1].astype(BF16)], axis=0)
 
         def product(i, carry, flow=flow, rhs=rhs):
             rows = pl.ds(pl.multiple_of(i * 128, 128), 128)
-            out = dot(tokx[flow, rows, :], rhs, ((1,), (0,)))
+            lhs = jnp.concatenate(
+                [tkr[flow, rows, :].astype(BF16), tkx[flow, rows, :].astype(BF16)], axis=1
+            )
+            out = dot(lhs, rhs, ((1,), (0,)))
             start = place_of(flow, bits_of(0, 0, i))
             for cx in range(NX):
                 for cy in range(NY):
@@ -450,8 +514,11 @@
         put(flow, other, 1 - bit, fr[flow, 1])
         put(flow, other, bit, fr[flow, 2])
 
-    for copy in [send_tok, pair_state, pair_scan] + tokens_out + relays + first + second + steps:
+    for copy in [send_tok] + pair_state + pair_scan + steps:
         copy.wait_send()
+    for copies in [tokens_out.values(), relays.values()] + first + second:
+        for copy in copies:
+            copy.wait_send()
     for flow in range(FLOWS):
         for copy in gather[flow] + handed[flow]:
             copy.wait_send()
@@ -466,7 +533,7 @@
     factor = 1.0 / math.sqrt(data_count * rows * seq_count)
     any_space = pl.BlockSpec(memory_space=pl.ANY)
     vmem = pl.BlockSpec(memory_space=pltpu.VMEM)
-    slices = (CHIPS, 64, HD)
+    slices = (CHUNKS, CHIPS, SLICE, HD)
     dma = pltpu.SemaphoreType.DMA
     token_grad, proj_grad = pl.pallas_call(
         functools.partial(kernel, scale, factor),
@@ -485,7 +552,6 @@
             pltpu.VMEM((FLOWS + 1, WIDTH, ROWS), F32),
             pltpu.VMEM((FLOWS, WIDTH, ROWS), F32),
             pltpu.VMEM((WIDTH, 2 * ROWS), BF16),
-            pltpu.VMEM((FLOWS, WIDTH, 2 * ROWS), BF16),
             pltpu.VMEM((2,) + slices, F32),
             pltpu.VMEM(slices, F32),
             pltpu.VMEM(slices, F32),
@@ -503,14 +569,14 @@
             pltpu.VMEM((FLOWS, 2, 8, HD), F32),
             pltpu.VMEM((FLOWS, 3, 8, HD), F32),
             dma((5,)),
-            dma((3,)),
-            dma((3,)),
-            dma((2 * FLOWS,)),
-            dma((2 * FLOWS,)),
-            dma((CHIPS - 1,)),
-            dma((CHIPS - 1,)),
-            dma((CHIPS - 1,)),
-            dma((CHIPS - 1,)),
+            dma((5,)),
+            dma((5,)),
+            dma((2 * FLOWS, 2)),
+            dma((2 * FLOWS, 2)),
+            dma((CHUNKS, CHIPS - 1)),
+            dma((CHUNKS, CHIPS - 1)),
+            dma((CHUNKS, CHIPS - 1)),
+            dma((CHUNKS, CHIPS - 1)),
             dma((FLOWS, 3)),
             dma((FLOWS, 3)),
             dma((FLOWS, STEPS)),

time: 88.5 us -> 87.5 us (0.989)
  Pallas kernels: 84.7 us -> 83.6 us
    pallas_call x1, Pallas kernels: 84.7 us -> 83.6 us  [shards(): pl.pallas_call(functools.partial(kernel, scale, factor), out_shape=(jax.S...]
where the time goes in v3:
time: 87.5 us; the launch traced here: 87.3 us
  Pallas kernels  83.6 us (96%)
  local copies, waits for them, and re-layouts  3.09 us (4%)
    pallas_call x1, Pallas kernels, shards(): pl.pallas_call(functools.partial(kernel, scale, factor), out_shape=(jax.S...  83.6 us
    unnamed x2, local copies, waits for them, and re-layouts  3.09 us

profile of v3, /device:TPU:1, one launch (start us, length us, event | category | flops | bytes accessed | tf_op | source)
XLA Modules:
  0.0 87.3 jit_solution(5910553387932009892)
XLA Ops:
  0.6 83.6 %shard_map.50 = (bf16[128,1024]{1,0:T(8,128)(2,1)}, f32[4,3072]{1,0:T(4,128)}) custom-call(bf16[128,1024]{1,0:T(8,128)(2,1)} %bitcast.4, bf16[1024,3072]{1,0:T(8,128)(2,1)} %w_hbm.1, bf16[128,1024]{1,0:T(8,128)(2,1)} %bitcast.5), custom_call_target="tpu_custom_call" | custom-call | tf_op jit(solution)/shard_map/pallas_call | solution.py:538
  84.2 1.7 %copy.7 = bf16[1,128,1024]{2,1,0:T(8,128)(2,1)} copy(bf16[1,128,1024]{2,1,0:T(8,128)(2,1)} %bitcast.3) | data formatting | bytes 524288
  85.9 1.4 %copy.8 = f32[4,3072]{1,0:T(4,128)} copy(f32[4,3072]{1,0:T(4,128)} %get-tuple-element.9) | data formatting | bytes 98304

commit v4 on v3

--- a/solution.py
+++ b/solution.py
@@ -23,13 +23,15 @@
 SLICE = 32
 FLOWS = 6
 GROUPS = 128
-STEPS = 6
+STEPS = 4
+OWNERS = 8
+PIECES = 4
 
 ORDERS = (
     ("xu", "xv", "yu", "yv", "za", "zb", "zc"),
-    ("xv", "xu", "yv", "yu", "zb", "za", "zc"),
-    ("yu", "yv", "za", "zb", "xu", "xv", "zc"),
-    ("yv", "yu", "zb", "za", "xv", "xu", "zc"),
+    ("xv", "xu", "yv", "yu", "za", "zb", "zc"),
+    ("yu", "yv", "xu", "xv", "za", "zb", "zc"),
+    ("yv", "yu", "xv", "xu", "za", "zb", "zc"),
     ("zb", "za", "xv", "xu", "yv", "yu", "zc"),
     ("za", "zb", "xu", "xv", "yu", "yv", "zc"),
 )
@@ -95,6 +97,7 @@
     acc,
     rb,
     fin,
+    finp,
     fr,
     load_sem,
     pair_send,
@@ -133,10 +136,35 @@
         "zb": ((z + 2 * (z % 2) - 1 + NZ) % NZ, seq),
         "zc": ((z + 4) % NZ, seq),
     }
-    home = dict(near, zb=((z // 4) * 4 + 3 - z % 4, seq))
-
     def crossed(device):
         return (device[0], device[1] + 1 - 2 * core)
+
+    def flipped_place(place, name):
+        px, py, pz = place
+        if name == "xu":
+            return (px + 1 - 2 * (px % 2), py, pz)
+        if name == "xv":
+            return (3 - px, py, pz)
+        if name == "yu":
+            return (px, py + 1 - 2 * (py % 2), pz)
+        if name == "yv":
+            return (px, 3 - py, pz)
+        if name == "za":
+            return (px, py, pz + 1 - 2 * (pz % 2))
+        if name == "zb":
+            return (px, py, (pz // 4) * 4 + 3 - pz % 4)
+        return (px, py, (pz + 4) % NZ)
+
+    def owners(flow):
+        first, left, right = ORDERS[flow][0], ORDERS[flow][5], ORDERS[flow][6]
+        found = []
+        for mask in range(OWNERS):
+            place = (x, y, z)
+            for name, on in ((first, mask & 1), (left, mask & 2), (right, mask & 4)):
+                if on:
+                    place = flipped_place(place, name)
+            found.append(place)
+        return found
 
     bits = bits_of(x, y, z)
     targets = []
@@ -167,9 +195,18 @@
     load_g.start()
 
     barrier = pltpu.get_barrier_semaphore()
-    greeted = [partner, near["za"], near["zb"], near["zc"]] + [t[1] for t in targets]
+    greeted = [partner] + [t[1] for t in targets]
     greeted += [crossed(near[order[0]]) for order in ORDERS]
-    greeted += [home["zb"], crossed(home["zb"])]
+    seen = set()
+    for flow in range(FLOWS):
+        first, left, right = ORDERS[flow][0], ORDERS[flow][5], ORDERS[flow][6]
+        for mask, place in enumerate(owners(flow)):
+            flips = [n for n, on in ((first, mask & 1), (left, mask & 2), (right, mask & 4)) if on]
+            key = frozenset(flips)
+            if any(name[0] == "z" for name in flips) and key not in seen:
+                seen.add(key)
+                greeted.append((place[2], seq_at(place[0], place[1])))
+    greeted.append(near["zb"])
     for device in greeted:
         pl.semaphore_signal(barrier, inc=1, device_id=device, device_id_type=MESH)
 
@@ -199,12 +236,12 @@
         return pl.ds(pl.multiple_of(part * INNER + h * HD, HD), HD)
 
     pl.semaphore_wait(barrier, len(greeted))
-    half = WIDTH // 2
+    piece = WIDTH // PIECES
     tokens_out = {}
     relays = {}
 
     def send_tokens(flows, part):
-        rows = pl.ds(part * half, half)
+        rows = pl.ds(part * piece, piece)
         for flow in flows:
             copy = remote(
                 tokf.at[rows],
@@ -217,7 +254,7 @@
             tokens_out[flow, part] = copy
 
     def relay_tokens(flows, part):
-        rows = pl.ds(part * half, half)
+        rows = pl.ds(part * piece, piece)
         for flow in flows:
             tokens_out[flow, part].wait_recv()
             copy = remote(
@@ -231,8 +268,9 @@
             relays[flow, part] = copy
 
     z_flows, xy_flows = (4, 5), (0, 1, 2, 3)
-    send_tokens(z_flows, 0)
-    send_tokens(z_flows, 1)
+    send_tokens(xy_flows, 0)
+    for part in range(PIECES):
+        send_tokens(z_flows, part)
 
     pair_state = []
     for chunk in range(CHUNKS):
@@ -275,7 +313,7 @@
             copies.append(copy)
         first.append(copies)
         r1[chunk, chip] = tb[chunk, chip]
-    send_tokens(xy_flows, 0)
+    send_tokens(xy_flows, 1)
     send_tok = remote(tokf, tkr.at[FLOWS], pair_send.at[4], pair_recv.at[4], partner)
     send_tok.start()
 
@@ -321,10 +359,11 @@
         second.append(copies)
         r2[chunk, chip] = eb[chunk, chip]
 
-    send_tokens(xy_flows, 1)
-    relay_tokens(z_flows, 0)
-    relay_tokens(z_flows, 1)
+    send_tokens(xy_flows, 2)
+    send_tokens(xy_flows, 3)
     relay_tokens(xy_flows, 0)
+    for part in range(PIECES):
+        relay_tokens(z_flows, part)
     send_tok.wait_recv()
     tokt[:, 128:256] = tkr[FLOWS].astype(BF16)
 
@@ -393,7 +432,8 @@
                 copies.append(copy)
             gather[flow] = copies
 
-    relay_tokens(xy_flows, 1)
+    for part in (1, 2, 3):
+        relay_tokens(xy_flows, part)
 
     def chip_part(pair):
         blocks = []
@@ -404,20 +444,15 @@
             blocks.append(jnp.concatenate([own, qr[flow, 2].astype(BF16)], axis=0))
         rhs = jnp.concatenate(blocks, axis=1)
 
-        def chip_product(i, carry):
-            rows = pl.ds(pl.multiple_of(i * 128, 128), 128)
-            out = dot(tokt[rows, :], rhs, ((1,), (0,)))
+        for i in range(NZ):
+            out = dot(tokt[i * 128 : i * 128 + 128, :], rhs, ((1,), (0,)))
             for part in range(3):
                 flow = 2 * part + pair
-                start = place_of(flow, bits_of(0, 0, i))
                 for cx in range(NX):
                     for cy in range(NY):
                         at = 8 * (cx * NY + cy)
                         block = out[at : at + 8, part * 128 : part * 128 + 128]
-                        acc[flow, start + place_of(flow, bits_of(cx, cy, 0))] = block
-            return carry
-
-        lax.fori_loop(0, NZ, chip_product, 0)
+                        acc[flow, place_of(flow, bits_of(cx, cy, i))] = block
 
     def halving(flow, step, base):
         size = GROUPS >> (step + 1)
@@ -437,27 +472,24 @@
     for flow in flow_order:
         if flow in (4, 5):
             chip_part(flow % 2)
-        relays[flow, 0].wait_recv()
-        relays[flow, 1].wait_recv()
+        for part in range(PIECES):
+            relays[flow, part].wait_recv()
         gather[flow][0].wait_recv()
         gather[flow][1].wait_recv()
         rhs = jnp.concatenate([qr[flow, 0].astype(BF16), qr[flow, 1].astype(BF16)], axis=0)
 
-        def product(i, carry, flow=flow, rhs=rhs):
-            rows = pl.ds(pl.multiple_of(i * 128, 128), 128)
+        for i in range(NZ):
+            rows = pl.ds(i * 128, 128)
             lhs = jnp.concatenate(
                 [tkr[flow, rows, :].astype(BF16), tkx[flow, rows, :].astype(BF16)], axis=1
             )
             out = dot(lhs, rhs, ((1,), (0,)))
-            start = place_of(flow, bits_of(0, 0, i))
             for cx in range(NX):
                 for cy in range(NY):
                     at = 8 * (cx * NY + cy)
-                    place = start + place_of(flow, bits_of(cx, cy, 0))
+                    place = place_of(flow, bits_of(cx, cy, i))
                     acc[flow, place] = acc[flow, place] + out[at : at + 8]
-            return carry
-
-        lax.fori_loop(0, NZ, product, 0)
+
         current[flow] = halving(flow, 0, 0)
         current[flow].start()
         steps.append(current[flow])
@@ -470,17 +502,18 @@
     lax.fori_loop(0, WIDTH // 256, token_rows, 0)
 
     def hand_out(flow):
-        bit = first_bit[flow]
-        device = home[ORDERS[flow][0]]
-        fin[flow, 0] = acc[flow, base[flow] + bit] * factor
-        fin[flow, 1] = acc[flow, base[flow] + 1 - bit] * factor
-        copies = []
-        for i, (src, to) in enumerate(((1, device), (1, crossed(device)), (0, partner))):
-            copy = remote(
-                fin.at[flow, src], fr.at[flow, i], f_send.at[flow, i], f_recv.at[flow, i], to
-            )
-            copy.start()
-            copies.append(copy)
+        copies = [None]
+        for mask, place in enumerate(owners(flow)):
+            if mask:
+                copy = remote(
+                    acc.at[flow, place_of(flow, bits_of(*place))],
+                    fr.at[flow, mask],
+                    f_send.at[flow, mask],
+                    f_recv.at[flow, mask],
+                    (place[2], seq_at(place[0], place[1])),
+                )
+                copy.start()
+                copies.append(copy)
         return copies
 
     handed = [None] * FLOWS
@@ -498,29 +531,35 @@
             else:
                 handed[flow] = hand_out(flow)
 
+    for flow in flow_order:
+        own = acc[flow, place_of(flow, bits)]
+        for copy in handed[flow][1:]:
+            copy.wait_recv()
+        fin[flow, 0] = (own + fr[flow, 2] + (fr[flow, 4] + fr[flow, 6])) * factor
+        fin[flow, 1] = ((fr[flow, 1] + fr[flow, 3]) + (fr[flow, 5] + fr[flow, 7])) * factor
+
+    last = remote(fin, finp, pair_send.at[5], pair_recv.at[5], partner)
+    last.start()
     low = core == 0
 
-    def put(flow, at_core, bit, rows):
-        cols = head_cols(flow // 2, head_of(flow, at_core, bit))
-        pg_ref[:, cols] = jnp.where(low, rows[0:4], rows[4:8])
-
-    for flow in flow_order:
-        put(flow, core, first_bit[flow], fin[flow, 0])
-    for flow in flow_order:
-        bit = first_bit[flow]
-        for copy in handed[flow]:
-            copy.wait_recv()
-        put(flow, core, 1 - bit, fr[flow, 0])
-        put(flow, other, 1 - bit, fr[flow, 1])
-        put(flow, other, bit, fr[flow, 2])
-
-    for copy in [send_tok] + pair_state + pair_scan + steps:
+    def put(at_core, source):
+        for flow in range(FLOWS):
+            for flip in range(2):
+                bit = first_bit[flow] + flip * (1 - 2 * first_bit[flow])
+                cols = head_cols(flow // 2, head_of(flow, at_core, bit))
+                pg_ref[:, cols] = jnp.where(low, source[flow, flip, 0:4], source[flow, flip, 4:8])
+
+    put(core, fin)
+    last.wait_recv()
+    put(other, finp)
+
+    for copy in [send_tok, last] + pair_state + pair_scan + steps:
         copy.wait_send()
     for copies in [tokens_out.values(), relays.values()] + first + second:
         for copy in copies:
             copy.wait_send()
     for flow in range(FLOWS):
-        for copy in gather[flow] + handed[flow]:
+        for copy in gather[flow] + handed[flow][1:]:
             copy.wait_send()
 
 
@@ -567,12 +606,13 @@
             pltpu.VMEM((FLOWS, GROUPS, 8, HD), F32),
             pltpu.VMEM((FLOWS, GROUPS, 8, HD), F32),
             pltpu.VMEM((FLOWS, 2, 8, HD), F32),
-            pltpu.VMEM((FLOWS, 3, 8, HD), F32),
+            pltpu.VMEM((FLOWS, 2, 8, HD), F32),
+            pltpu.VMEM((FLOWS, OWNERS, 8, HD), F32),
             dma((5,)),
-            dma((5,)),
-            dma((5,)),
-            dma((2 * FLOWS, 2)),
-            dma((2 * FLOWS, 2)),
+            dma((6,)),
+            dma((6,)),
+            dma((2 * FLOWS, PIECES)),
+            dma((2 * FLOWS, PIECES)),
             dma((CHUNKS, CHIPS - 1)),
             dma((CHUNKS, CHIPS - 1)),
             dma((CHUNKS, CHIPS - 1)),
@@ -581,8 +621,8 @@
             dma((FLOWS, 3)),
             dma((FLOWS, STEPS)),
             dma((FLOWS, STEPS)),
-            dma((FLOWS, 3)),
-            dma((FLOWS, 3)),
+            dma((FLOWS, OWNERS)),
+            dma((FLOWS, OWNERS)),
         ],
         compiler_params=pltpu.CompilerParams(
             collective_id=0, has_side_effects=True, vmem_limit_bytes=60 * 1024 * 1024

time: 87.5 us -> 78.7 us (0.90)
  Pallas kernels: 83.6 us -> 74.9 us
    pallas_call x1, Pallas kernels: 83.6 us -> 74.9 us  [shards(): pl.pallas_call(functools.partial(kernel, scale, factor), out_shape=(jax.S...]
where the time goes in v4:
time: 78.7 us; the launch traced here: 78.6 us
  Pallas kernels  74.9 us (95%)
  local copies, waits for them, and re-layouts  3.09 us (4%)
    pallas_call x1, Pallas kernels, shards(): pl.pallas_call(functools.partial(kernel, scale, factor), out_shape=(jax.S...  74.9 us
    unnamed x2, local copies, waits for them, and re-layouts  3.09 us

profile of v4, /device:TPU:1, one launch (start us, length us, event | category | flops | bytes accessed | tf_op | source)
XLA Modules:
  0.0 78.6 jit_solution(3308778635912713103)
XLA Ops:
  0.6 74.9 %shard_map.50 = (bf16[128,1024]{1,0:T(8,128)(2,1)}, f32[4,3072]{1,0:T(4,128)}) custom-call(bf16[128,1024]{1,0:T(8,128)(2,1)} %bitcast.4, bf16[1024,3072]{1,0:T(8,128)(2,1)} %w_hbm.1, bf16[128,1024]{1,0:T(8,128)(2,1)} %bitcast.5), custom_call_target="tpu_custom_call" | custom-call | tf_op jit(solution)/shard_map/pallas_call | solution.py:577
  75.5 1.7 %copy.7 = bf16[1,128,1024]{2,1,0:T(8,128)(2,1)} copy(bf16[1,128,1024]{2,1,0:T(8,128)(2,1)} %bitcast.3) | data formatting | bytes 524288
  77.2 1.4 %copy.8 = f32[4,3072]{1,0:T(4,128)} copy(f32[4,3072]{1,0:T(4,128)} %get-tuple-element.9) | data formatting | bytes 98304

commit v5 on v4

--- a/solution.py
+++ b/solution.py
@@ -195,18 +195,8 @@
     load_g.start()
 
     barrier = pltpu.get_barrier_semaphore()
-    greeted = [partner] + [t[1] for t in targets]
+    greeted = [partner, near["za"], near["zb"]] + [t[1] for t in targets]
     greeted += [crossed(near[order[0]]) for order in ORDERS]
-    seen = set()
-    for flow in range(FLOWS):
-        first, left, right = ORDERS[flow][0], ORDERS[flow][5], ORDERS[flow][6]
-        for mask, place in enumerate(owners(flow)):
-            flips = [n for n, on in ((first, mask & 1), (left, mask & 2), (right, mask & 4)) if on]
-            key = frozenset(flips)
-            if any(name[0] == "z" for name in flips) and key not in seen:
-                seen.add(key)
-                greeted.append((place[2], seq_at(place[0], place[1])))
-    greeted.append(near["zb"])
     for device in greeted:
         pl.semaphore_signal(barrier, inc=1, device_id=device, device_id_type=MESH)
 
@@ -275,17 +265,15 @@
     pair_state = []
     for chunk in range(CHUNKS):
 
-        def local_state(i, carry, chunk=chunk):
+        for i in range(HEADS // CHUNKS):
             h = 4 * chunk + i
             q = proj[:, head_cols(0, h)]
             k = proj[:, head_cols(1, h)]
             v = proj[:, head_cols(2, h)]
             d = g[:, head_cols(0, h)]
-            loc[0, chunk, pl.ds(4 * i, 4)] = dot(k, v, ((0,), (0,))).reshape(4, SLICE, HD)
-            loc[1, chunk, pl.ds(4 * i, 4)] = (scale * dot(q, d, ((0,), (0,)))).reshape(4, SLICE, HD)
-            return carry
-
-        lax.fori_loop(0, HEADS // CHUNKS, local_state, 0)
+            loc[0, chunk, 4 * i : 4 * i + 4] = dot(k, v, ((0,), (0,))).reshape(4, SLICE, HD)
+            loc[1, chunk, 4 * i : 4 * i + 4] = (scale * dot(q, d, ((0,), (0,)))).reshape(4, SLICE, HD)
+
         copy = remote(
             loc.at[core, chunk],
             s1b.at[chunk],
@@ -468,9 +456,9 @@
     base = [0] * FLOWS
     steps = []
     current = [None] * FLOWS
-    flow_order = (4, 2, 0, 5, 3, 1)
+    flow_order = (2, 0, 4, 5, 3, 1)
     for flow in flow_order:
-        if flow in (4, 5):
+        if flow in (2, 5):
             chip_part(flow % 2)
         for part in range(PIECES):
             relays[flow, part].wait_recv()
@@ -519,7 +507,7 @@
     handed = [None] * FLOWS
     for step in range(STEPS):
         size = GROUPS >> (step + 1)
-        for flow in flow_order:
+        for flow in flow_order if step + 1 < STEPS else (2, 0, 3, 1, 4, 5):
             current[flow].wait_recv()
             base[flow] = base[flow] + bits[ORDERS[flow][step + 1]] * size
             kept = pl.ds(base[flow], size)

time: 78.7 us -> 79.3 us (level)
  no operation moved by 1% of the time
where the time goes in v5:
time: 79.3 us; the launch traced here: 79.1 us
  Pallas kernels  75.4 us (95%)
  local copies, waits for them, and re-layouts  3.09 us (4%)
    pallas_call x1, Pallas kernels, shards(): pl.pallas_call(functools.partial(kernel, scale, factor), out_shape=(jax.S...  75.4 us
    unnamed x2, local copies, waits for them, and re-layouts  3.09 us

profile of v5, /device:TPU:1, one launch (start us, length us, event | category | flops | bytes accessed | tf_op | source)
XLA Modules:
  0.0 79.1 jit_solution(4095154529912192956)
XLA Ops:
  0.6 75.4 %shard_map.50 = (bf16[128,1024]{1,0:T(8,128)(2,1)}, f32[4,3072]{1,0:T(4,128)}) custom-call(bf16[128,1024]{1,0:T(8,128)(2,1)} %bitcast.4, bf16[1024,3072]{1,0:T(8,128)(2,1)} %w_hbm.1, bf16[128,1024]{1,0:T(8,128)(2,1)} %bitcast.5), custom_call_target="tpu_custom_call" | custom-call | tf_op jit(solution)/shard_map/pallas_call | solution.py:565
  76.0 1.7 %copy.7 = bf16[1,128,1024]{2,1,0:T(8,128)(2,1)} copy(bf16[1,128,1024]{2,1,0:T(8,128)(2,1)} %bitcast.3) | data formatting | bytes 524288
  77.7 1.4 %copy.8 = f32[4,3072]{1,0:T(4,128)} copy(f32[4,3072]{1,0:T(4,128)} %get-tuple-element.9) | data formatting | bytes 98304

commit v6 on v5

--- a/solution.py
+++ b/solution.py
@@ -219,7 +219,7 @@
             proj[:, cols] = dot(tok[...], w[:, cols], ((1,), (0,))).astype(BF16)
             return carry
 
-        lax.fori_loop(0, INNER // 256, project, 0)
+        lax.fori_loop(0, INNER // 256, project, 0, unroll=True)
     load_g.wait()
 
     def head_cols(part, h):
@@ -549,6 +549,24 @@
     for flow in range(FLOWS):
         for copy in gather[flow] + handed[flow][1:]:
             copy.wait_send()
+
+
+def settle(tg_in, pg_in, tg_out, pg_out, tg, pg, sem_in, sem_out):
+    ins = [
+        pltpu.make_async_copy(tg_in, tg, sem_in.at[0]),
+        pltpu.make_async_copy(pg_in, pg, sem_in.at[1]),
+    ]
+    outs = [
+        pltpu.make_async_copy(tg, tg_out, sem_out.at[0]),
+        pltpu.make_async_copy(pg, pg_out, sem_out.at[1]),
+    ]
+    for copy in ins:
+        copy.start()
+    for copy, out in zip(ins, outs):
+        copy.wait()
+        out.start()
+    for out in outs:
+        out.wait()
 
 
 def shards(tokens, weights, dout):
@@ -616,6 +634,21 @@
             collective_id=0, has_side_effects=True, vmem_limit_bytes=60 * 1024 * 1024
         ),
     )(tokens.reshape(rows, width), weights, dout.reshape(rows, INNER))
+    token_grad, proj_grad = pl.pallas_call(
+        settle,
+        out_shape=(
+            jax.ShapeDtypeStruct((rows, width), BF16),
+            jax.ShapeDtypeStruct((4, 3 * INNER), F32),
+        ),
+        in_specs=[any_space] * 2,
+        out_specs=(any_space, any_space),
+        scratch_shapes=[
+            pltpu.VMEM((rows, width), BF16),
+            pltpu.VMEM((4, 3 * INNER), F32),
+            dma((2,)),
+            dma((2,)),
+        ],
+    )(token_grad, proj_grad)
     return (token_grad.reshape(1, rows, width), proj_grad)
 
 

time: 79.3 us -> 76.9 us (0.970)
  local copies, waits for them, and re-layouts: 3.09 us -> 0 us
  Pallas kernels: 75.4 us -> 76.2 us
    unnamed x2 -> x0, local copies, waits for them, and re-layouts: 3.09 us -> none
    pallas_call x0 -> x1, Pallas kernels: none -> 1.69 us  [shards(): pl.pallas_call(settle, out_shape=(jax.ShapeDtypeStruct((rows, width), BF1...]
    pallas_call x1, Pallas kernels: 75.4 us -> 74.5 us  [shards(): pl.pallas_call(functools.partial(kernel, scale, factor), out_shape=(jax.S...]
where the time goes in v6:
time: 76.9 us; the launch traced here: 76.8 us
  Pallas kernels  76.2 us (99%)
    pallas_call x1, Pallas kernels, shards(): pl.pallas_call(functools.partial(kernel, scale, factor), out_shape=(jax.S...  74.5 us
    pallas_call x1, Pallas kernels, shards(): pl.pallas_call(settle, out_shape=(jax.ShapeDtypeStruct((rows, width), BF1...  1.69 us

profile of v6, /device:TPU:1, one launch (start us, length us, event | category | flops | bytes accessed | tf_op | source)
XLA Modules:
  0.0 76.8 jit_solution(3669162946222833412)
XLA Ops:
  0.6 74.5 %shard_map.50 = (bf16[128,1024]{1,0:T(8,128)(2,1)}, f32[4,3072]{1,0:T(4,128)}) custom-call(bf16[128,1024]{1,0:T(8,128)(2,1)} %bitcast.3, bf16[1024,3072]{1,0:T(8,128)(2,1)} %w_hbm.1, bf16[128,1024]{1,0:T(8,128)(2,1)} %bitcast.4), custom_call_target="tpu_custom_call" | custom-call | tf_op jit(solution)/shard_map/pallas_call | solution.py:583
  75.1 1.7 %shard_map.51 = (bf16[128,1024]{1,0:T(8,128)(2,1)}, f32[4,3072]{1,0:T(4,128)}) custom-call(bf16[128,1024]{1,0:T(8,128)(2,1)} %get-tuple-element.6.tg_in, f32[4,3072]{1,0:T(4,128)} %get-tuple-element.7.pg_in), custom_call_target="tpu_custom_call" | custom-call | tf_op jit(solution)/shard_map/pallas_call | solution.py:637

commit v7 on v6

--- a/solution.py
+++ b/solution.py
@@ -30,8 +30,8 @@
 ORDERS = (
     ("xu", "xv", "yu", "yv", "za", "zb", "zc"),
     ("xv", "xu", "yv", "yu", "za", "zb", "zc"),
-    ("yu", "yv", "xu", "xv", "za", "zb", "zc"),
-    ("yv", "yu", "xv", "xu", "za", "zb", "zc"),
+    ("yu", "yv", "za", "xu", "xv", "zb", "zc"),
+    ("yv", "yu", "zb", "xv", "xu", "za", "zc"),
     ("zb", "za", "xv", "xu", "yv", "yu", "zc"),
     ("za", "zb", "xu", "xv", "yu", "yv", "zc"),
 )
@@ -507,7 +507,7 @@
     handed = [None] * FLOWS
     for step in range(STEPS):
         size = GROUPS >> (step + 1)
-        for flow in flow_order if step + 1 < STEPS else (2, 0, 3, 1, 4, 5):
+        for flow in flow_order if step + 1 < STEPS else range(FLOWS):
             current[flow].wait_recv()
             base[flow] = base[flow] + bits[ORDERS[flow][step + 1]] * size
             kept = pl.ds(base[flow], size)

time: 76.9 us -> 75.8 us (0.986)
  Pallas kernels: 76.2 us -> 75 us
    pallas_call x1, Pallas kernels: 74.5 us -> 73.3 us  [shards(): pl.pallas_call(functools.partial(kernel, scale, factor), out_shape=(jax.S...]
where the time goes in v7:
time: 75.8 us; the launch traced here: 75.7 us
  Pallas kernels  75 us (99%)
    pallas_call x1, Pallas kernels, shards(): pl.pallas_call(functools.partial(kernel, scale, factor), out_shape=(jax.S...  73.3 us
    pallas_call x1, Pallas kernels, shards(): pl.pallas_call(settle, out_shape=(jax.ShapeDtypeStruct((rows, width), BF1...  1.69 us

profile of v7, /device:TPU:1, one launch (start us, length us, event | category | flops | bytes accessed | tf_op | source)
XLA Modules:
  0.0 75.7 jit_solution(11671144902443509822)
XLA Ops:
  0.6 73.3 %shard_map.50 = (bf16[128,1024]{1,0:T(8,128)(2,1)}, f32[4,3072]{1,0:T(4,128)}) custom-call(bf16[128,1024]{1,0:T(8,128)(2,1)} %bitcast.3, bf16[1024,3072]{1,0:T(8,128)(2,1)} %w_hbm.1, bf16[128,1024]{1,0:T(8,128)(2,1)} %bitcast.4), custom_call_target="tpu_custom_call" | custom-call | tf_op jit(solution)/shard_map/pallas_call | solution.py:583
  74.0 1.7 %shard_map.51 = (bf16[128,1024]{1,0:T(8,128)(2,1)}, f32[4,3072]{1,0:T(4,128)}) custom-call(bf16[128,1024]{1,0:T(8,128)(2,1)} %get-tuple-element.6.tg_in, f32[4,3072]{1,0:T(4,128)} %get-tuple-element.7.pg_in), custom_call_target="tpu_custom_call" | custom-call | tf_op jit(solution)/shard_map/pallas_call | solution.py:637

commit v8 on v7

--- a/solution.py
+++ b/solution.py
@@ -487,12 +487,13 @@
         tg_ref[:, rows] = dot(qg[...], w[rows, :], ((1,), (1,))).astype(BF16)
         return carry
 
-    lax.fori_loop(0, WIDTH // 256, token_rows, 0)
 
     def hand_out(flow):
         copies = [None]
-        for mask, place in enumerate(owners(flow)):
+        places = owners(flow)
+        for mask in (7, 5, 6, 4, 3, 2, 1):
             if mask:
+                place = places[mask]
                 copy = remote(
                     acc.at[flow, place_of(flow, bits_of(*place))],
                     fr.at[flow, mask],
@@ -506,6 +507,7 @@
 
     handed = [None] * FLOWS
     for step in range(STEPS):
+        token_rows(step, 0)
         size = GROUPS >> (step + 1)
         for flow in flow_order if step + 1 < STEPS else range(FLOWS):
             current[flow].wait_recv()

time: 75.8 us -> 75.7 us (level)
  no operation moved by 1% of the time
where the time goes in v8:
time: 75.7 us; the launch traced here: 75.6 us
  Pallas kernels  75 us (99%)
    pallas_call x1, Pallas kernels, shards(): pl.pallas_call(functools.partial(kernel, scale, factor), out_shape=(jax.S...  73.3 us
    pallas_call x1, Pallas kernels, shards(): pl.pallas_call(settle, out_shape=(jax.ShapeDtypeStruct((rows, width), BF1...  1.69 us

profile of v8, /device:TPU:1, one launch (start us, length us, event | category | flops | bytes accessed | tf_op | source)
XLA Modules:
  0.0 75.6 jit_solution(10155998262827410700)
XLA Ops:
  0.6 73.3 %shard_map.50 = (bf16[128,1024]{1,0:T(8,128)(2,1)}, f32[4,3072]{1,0:T(4,128)}) custom-call(bf16[128,1024]{1,0:T(8,128)(2,1)} %bitcast.3, bf16[1024,3072]{1,0:T(8,128)(2,1)} %w_hbm.1, bf16[128,1024]{1,0:T(8,128)(2,1)} %bitcast.4), custom_call_target="tpu_custom_call" | custom-call | tf_op jit(solution)/shard_map/pallas_call | solution.py:585
  73.9 1.7 %shard_map.51 = (bf16[128,1024]{1,0:T(8,128)(2,1)}, f32[4,3072]{1,0:T(4,128)}) custom-call(bf16[128,1024]{1,0:T(8,128)(2,1)} %get-tuple-element.6.tg_in, f32[4,3072]{1,0:T(4,128)} %get-tuple-element.7.pg_in), custom_call_target="tpu_custom_call" | custom-call | tf_op jit(solution)/shard_map/pallas_call | solution.py:639
